TPU v7x, 32 devices: a whole 2x2x4 slice. The times are simulated.
32 devices in a mesh: feat: 8 (over z, y), pair: 4 (over x, core).
Axes of the slice: x: 2, y: 2, z: 4, core: 2. Of those that a mesh axis runs over, the one named last changes fastest.
Arguments:
- in_factors: bfloat16 [512, 2, 512, 256], P(('feat', 'pair')), may hold values from -6 to 6
- out_factors: bfloat16 [512, 2, 512, 256], P(('feat', 'pair')), may hold values from -0.26367188 to 0.26367188
- token_counts: int32 [512, 2], P(('feat', 'pair')), may hold values from 1 to 512, as said below
- slot_pair: int32 [4, 128], P('pair'), may hold values from 0 to 127, each once within a row
- factor_panels: float32 [65536, 1536], P('feat'), as said below
Outputs:
- reduced: float32 [512, 65536], P('pair', 'feat')
Inputs may be any that keep to these rules, and one draw needn't show every extreme that they name: `token_counts`: column 0 counts the chosen response's tokens, column 1 the rejected one's; positions at or beyond the count are padding. `slot_pair`: each row is a permutation of 0 to 127. `factor_panels`: entries above the diagonal in the unknowns' order are zero: rows of panel j hold zeros in the columns of panels after j, and D_k has a positive diagonal.
All inputs are finite; a program needn't handle non-finite values.
Results may differ from a plain program's by a relative error of at most 0.0003.
Values sent between devices are 32-bit elements; how exact they have to be, the bound alone decides.
A program may use at most 128 MiB of HBM per device.

v0:
```python
import jax
import jax.numpy as jnp
from jax import lax
from jax.sharding import PartitionSpec as P

PANEL = 512
PANELS = 3


def spread(value, axis, source):
    kept = jnp.where(lax.axis_index(axis) == source, value, 0).astype(value.dtype)
    return lax.psum(kept, axis)


def panel_product(solved, panel_cols):
    return lax.dot_general(
        solved,
        panel_cols,
        (((1,), (1,)), ((), ())),
        precision=lax.Precision.HIGHEST,
        preferred_element_type=jnp.float32,
    )


def per_device(in_factors, out_factors, token_counts, slot_pair, factor_panels):
    slot_count, side_count, token_depth, proj_rank = in_factors.shape
    n_pair = lax.axis_size("pair")
    n_feat = lax.axis_size("feat")
    per_group = slot_count // n_pair
    row_count = factor_panels.shape[0]
    feat_index = lax.axis_index("feat")
    positions = lax.broadcasted_iota(jnp.int32, (slot_count, side_count, token_depth), 2)
    side_index = lax.broadcasted_iota(jnp.int32, (slot_count, side_count, token_depth), 1)
    weights = jnp.where(
        positions < token_counts[:, :, None], jnp.where(side_index == 0, 1.0, -1.0), 0.0
    ).astype(jnp.bfloat16)
    signed = out_factors * weights[..., None]
    gradients = jnp.einsum("ksti,kstj->kij", signed, in_factors, preferred_element_type=jnp.float32)
    gradients = gradients.reshape(n_pair, per_group, n_feat, row_count)
    group_pairs = slot_pair[0]
    pair_total = n_pair * n_feat * per_group
    outgoing = gradients.transpose(2, 0, 1, 3).reshape(n_feat * n_pair, per_group, row_count)
    received = lax.all_to_all(
        outgoing, ("feat", "pair"), split_axis=0, concat_axis=1, tiled=True
    ).reshape(pair_total, row_count)
    pair_rows = lax.broadcasted_iota(jnp.int32, (pair_total, pair_total), 0)
    placement = (pair_rows == group_pairs[None, :]).astype(jnp.float32)
    right_side = jnp.dot(
        placement, received, precision=lax.Precision.HIGHEST, preferred_element_type=jnp.float32
    )
    identity = jnp.eye(PANEL, dtype=jnp.float32)

    def solve_panel(k, current):
        diagonal = jnp.where(
            feat_index == k, factor_panels[:PANEL, k * PANEL : (k + 1) * PANEL], identity
        )
        solved = jax.scipy.linalg.solve_triangular(diagonal, current[:, :PANEL].T, lower=True).T
        return spread(solved, "feat", k)

    solved = solve_panel(0, right_side)
    for k in range(PANELS):
        panel_cols = factor_panels[:, k * PANEL : (k + 1) * PANEL]
        head_rows = right_side[:, :PANEL] - panel_product(solved, panel_cols[:PANEL])
        head_rows = jnp.where(feat_index == k, solved, head_rows)
        following = solved
        if k + 1 < PANELS:
            following = solve_panel(k + 1, head_rows)
        tail_rows = right_side[:, PANEL:] - panel_product(solved, panel_cols[PANEL:])
        right_side = jnp.concatenate([head_rows, tail_rows], axis=1)
        solved = following
    return right_side


def solution(mesh):
    return jax.shard_map(
        per_device,
        mesh=mesh,
        in_specs=(
            P(("feat", "pair"), None, None, None),
            P(("feat", "pair"), None, None, None),
            P(("feat", "pair"), None),
            P("pair", None),
            P("feat", None),
        ),
        out_specs=P("pair", "feat"),
        check_vma=False,
    )
```

profile of v0, /device:TPU:0, one launch (start us, length us, event | category | flops | bytes accessed | tf_op | source)
XLA Modules:
  0.0 420.1 jit_solution(17209154780739720358)
XLA Ops:
  6.5 0.8 copy.20
  7.4 9.8 %fusion.18 = f32[16,256,256]{2,1,0:T(8,128)} fusion(bf16[16,2,512,256]{3,2,1,0:T(8,128)(2,1)} %param.7, bf16[16,2,512,256]{3,2,1,0:T(8,128)(2,1)} %param.8, bf16[16,2,512]{2,1,0:T(2,128)(2,1)S(1)} %fusion.63), kind=kOutput, calls=%fused_computation.19 | convolution fusion | flops 2151677952 | bytes 21004288 | tf_op jit(solution)/shard_map/ksti,kstj->kij/dot_general | solution.py:38
  17.3 5.0 %reshape.28 = f32[4,4,8,8192]{3,2,1,0:T(8,128)} reshape(f32[16,256,256]{2,1,0:T(8,128)} %fusion.18) | data formatting | bytes 8388608 | tf_op jit(solution)/shard_map/reshape | solution.py:39
  22.2 6.9 %copy.22 = f32[4,4,8,8192]{3,1,0,2:T(4,128)} copy(f32[4,4,8,8192]{3,2,1,0:T(8,128)} %reshape.28) | data formatting | bytes 8388608 | tf_op jit(solution)/shard_map/reshape | solution.py:39
  29.1 7.5 %all-to-all-start = ((f32[32,4,8192]{2,1,0:T(4,128)}), f32[32,4,8192]{2,1,0:T(4,128)}, u32[]{:S(2)}, u32[]{:S(2)}) async-start(f32[32,4,8192]{2,1,0:T(4,128)} %bitcast.103), calls=%async_computation | async-start | bytes 8388608 | tf_op jit(solution)/shard_map/all_to_all | solution.py:43
  37.0 2.3 fusion.24
  39.3 8.4 %while.6 = (s32[]{:T(128)}, f32[512,512]{1,0:T(8,128)S(1)}, s32[4,2]{0,1:T(2,128)S(1)}, f32[4,128,128]{2,1,0:T(8,128)S(1)}, s32[]{:T(128)}) while((s32[]{:T(128)}, f32[512,512]{1,0:T(8,128)S(1)}, s32[4,2]{0,1:T(2,128)S(1)}, f32[4,128,128]{2,1,0:T(8,128)S(1)}, s32[]{:T(128)}) %tuple.51), condition=%wide.while_cond, body=%wide.while_body.sunk | while | flops 2 | bytes 131189 | solution.py:57
  39.4 0.6 fusion.116
  40.0 1.4 bitcast_dynamic-update-slice_fusion.6
  41.5 0.6 fusion.116
  42.1 1.4 bitcast_dynamic-update-slice_fusion.6
  43.6 0.6 fusion.116
  44.2 1.4 bitcast_dynamic-update-slice_fusion.6
  46.3 1.4 bitcast_dynamic-update-slice_fusion.6
  47.7 0.7 copy-done.4
  48.4 40.1 %custom-call.5 = f32[4,128,128]{1,2,0:T(8,128)S(1)} custom-call(f32[4,128,128]{2,1,0:T(8,128)} %copy-done.4), custom_call_target="InvertDiagBlocksLowerTriangular" | custom-call | tf_op jit(solution)/shard_map/jit(_solve_triangular)/triangular_solve | solution.py:57
  88.6 0.8 broadcast.62.clone.1
  89.3 9.7 %while.7 = (s32[]{:T(128)}, f32[512,512]{1,0:T(8,128)S(1)}, s32[4,2]{0,1:T(2,128)S(1)}, f32[4,128,128]{2,1,0:T(8,128)}, s32[]{:T(128)}) while((s32[]{:T(128)}, f32[512,512]{1,0:T(8,128)S(1)}, s32[4,2]{0,1:T(2,128)S(1)}, f32[4,128,128]{2,1,0:T(8,128)}, s32[]{:T(128)}) %tuple.66), condition=%wide.while_cond.clone, body=%wide.while_body.clone.sunk | while | flops 2 | bytes 132205 | solution.py:57
  89.9 1.8 bitcast_dynamic-update-slice_fusion.7
  92.3 1.8 bitcast_dynamic-update-slice_fusion.7
  94.8 1.8 bitcast_dynamic-update-slice_fusion.7
  97.2 1.8 bitcast_dynamic-update-slice_fusion.7
  99.0 31.2 %all-to-all-done = f32[32,4,8192]{2,1,0:T(4,128)} async-done(((f32[32,4,8192]{2,1,0:T(4,128)}), f32[32,4,8192]{2,1,0:T(4,128)}, u32[]{:S(2)}, u32[]{:S(2)}) %all-to-all-start) | async-done | bytes 4194336 | tf_op jit(solution)/shard_map/all_to_all | solution.py:43
  130.3 5.3 %reshape.30 = f32[128,8192]{1,0:T(8,128)} reshape(f32[32,4,8192]{2,1,0:T(4,128)} %all-to-all-done) | data formatting | bytes 8388608 | tf_op jit(solution)/shard_map/reshape | solution.py:45
  135.5 4.5 %fusion.82 = f32[128,8192]{1,0:T(8,128)S(1)} fusion(f32[128,8192]{1,0:T(8,128)} %reshape.30, s32[128]{0:T(128)S(1)} %bitcast.112), kind=kOutput, calls=%fused_computation.116 | convolution fusion | flops 1610629120 | bytes 8389120 | tf_op jit(solution)/shard_map/dot_general | solution.py:48
  140.1 2.0 copy-done
  143.4 1.1 fusion.77
  145.3 1.1 fusion.76
  146.4 0.7 fusion.30
  147.2 0.6 all-reduce.6.cloned.1.call-start
  147.8 7.8 %while.8 = (s32[]{:T(128)}, f32[512,512]{1,0:T(8,128)S(1)}, s32[4,2]{0,1:T(2,128)S(1)}, f32[4,128,128]{2,1,0:T(8,128)S(1)}, s32[]{:T(128)}) while((s32[]{:T(128)}, f32[512,512]{1,0:T(8,128)S(1)}, s32[4,2]{0,1:T(2,128)S(1)}, f32[4,128,128]{2,1,0:T(8,128)S(1)}, s32[]{:T(128)}) %tuple.67), condition=%wide.while_cond.clone.1, body=%wide.while_body.clone.1.sunk | while | flops 2 | bytes 131189 | solution.py:57
  148.5 1.3 bitcast_dynamic-update-slice_fusion.8
  150.4 1.3 bitcast_dynamic-update-slice_fusion.8
  152.4 1.3 bitcast_dynamic-update-slice_fusion.8
  154.3 1.3 bitcast_dynamic-update-slice_fusion.8
  155.6 40.1 %custom-call.6 = f32[4,128,128]{1,2,0:T(8,128)S(1)} custom-call(f32[4,128,128]{2,1,0:T(8,128)} %get-tuple-element.27), custom_call_target="InvertDiagBlocksLowerTriangular" | custom-call | tf_op jit(solution)/shard_map/jit(_solve_triangular)/triangular_solve | solution.py:57
  195.8 39.3 %custom-call.7 = f32[4,128,128]{1,2,0:T(8,128)S(1)} custom-call(f32[4,128,128]{2,1,0:T(8,128)S(1)} %get-tuple-element.28), custom_call_target="InvertDiagBlocksLowerTriangular" | custom-call | tf_op jit(solution)/shard_map/jit(_solve_triangular)/triangular_solve | solution.py:57
  235.1 2.6 fusion.23
  240.3 0.7 fusion.31
  241.3 21.2 %fusion.6 = f32[128,7680]{1,0:T(8,128)} fusion(f32[128,512]{1,0:T(8,128)S(1)} %copy-done.1, f32[8192,1536]{1,0:T(8,128)} %param.11, f32[128,8192]{1,0:T(8,128)} %copy-done), kind=kOutput, calls=%fused_computation.12 | convolution fusion | flops 6040780800 | bytes 23855104 | tf_op jit(solution)/shard_map/dot_general | solution.py:16
  262.5 49.2 %all-reduce.6.cloned.1.call-done = f32[128,512]{1,0:T(8,128)} async-done(((f32[128,512]{1,0:T(8,128)}), f32[128,512]{1,0:T(8,128)}) %all-reduce.6.cloned.1.call-update) | async-done | bytes 262160 | tf_op jit(solution)/shard_map/psum | solution.py:12
  311.7 2.6 fusion.22
  316.9 0.7 fusion.32
  317.6 23.0 %fusion.9 = f32[128,7680]{1,0:T(8,128)} fusion(f32[128,7680]{1,0:T(8,128)} %fusion.6, f32[128,512]{1,0:T(8,128)S(1)} %copy-done.2, f32[8192,1536]{1,0:T(8,128)} %param.11), kind=kOutput, calls=%fused_computation.13 | convolution fusion | flops 6040780800 | bytes 23855104 | tf_op jit(solution)/shard_map/dot_general | solution.py:16
  340.6 47.4 %all-reduce.8.cloned.1.call-done = f32[128,512]{1,0:T(8,128)} async-done(((f32[128,512]{1,0:T(8,128)}), f32[128,512]{1,0:T(8,128)}) %all-reduce.8.cloned.1.call-update) | async-done | bytes 262160 | tf_op jit(solution)/shard_map/psum | solution.py:12
  388.0 2.5 fusion.21
  390.5 20.4 %fusion.12 = f32[128,7680]{1,0:T(8,128)S(1)} fusion(f32[128,7680]{1,0:T(8,128)} %fusion.9, f32[128,512]{1,0:T(8,128)} %all-reduce.8.cloned.1.call-done, f32[8192,1536]{1,0:T(8,128)} %param.11), kind=kOutput, calls=%fused_computation.14 | convolution fusion | flops 6040780800 | bytes 23855104 | tf_op jit(solution)/shard_map/dot_general | solution.py:16
  411.0 2.3 pad_maximum_fusion
  (72 shorter events, 13.8 us)
Async XLA Ops:
  29.1 101.2 %all-to-all-start = ((f32[32,4,8192]{2,1,0:T(4,128)}), f32[32,4,8192]{2,1,0:T(4,128)}, u32[]{:S(2)}, u32[]{:S(2)}) async-start(f32[32,4,8192]{2,1,0:T(4,128)} %bitcast.103), calls=%async_computation | async-start | bytes 8388608 | tf_op jit(solution)/shard_map/all_to_all | solution.py:43
  36.6 198.5 %all-reduce.4.cloned.1.call-start = ((), (), s32[]{:S(2)}) async-start(), calls=%async_computation.1 | async-start | bytes 524288 | tf_op jit(solution)/shard_map/psum | solution.py:12
  47.7 0.7 copy-start.4
  88.6 54.2 %copy-start.3 = (f32[4,128,128]{1,2,0:T(8,128)}, f32[4,128,128]{1,2,0:T(8,128)S(1)}, u32[]{:S(2)}) copy-start(f32[4,128,128]{1,2,0:T(8,128)S(1)} %custom-call.5) | copy-start | bytes 786436
  99.0 36.5 %copy-start.5 = (s32[1,128]{1,0:T(1,128)S(1)}, s32[1,128]{1,0:T(1,128)}, u32[]{:S(2)}) copy-start(s32[1,128]{1,0:T(1,128)} %param.10) | copy-start | bytes 1540
  140.1 2.0 copy-start
  147.2 164.6 %all-reduce.6.cloned.1.call-start = ((), (), s32[]{:S(2)}) async-start(), calls=%async_computation.2 | async-start | bytes 524288 | tf_op jit(solution)/shard_map/psum | solution.py:12
  235.1 6.2 %copy-start.1 = (f32[128,512]{1,0:T(8,128)S(1)}, f32[128,512]{1,0:T(8,128)}, u32[]{:S(2)}) copy-start(f32[128,512]{1,0:T(8,128)} %all-reduce.4.cloned.1.call-done) | copy-start | bytes 786436
  241.1 146.9 %all-reduce.8.cloned.1.call-start = ((), (), s32[]{:S(2)}) async-start(), calls=%async_computation.3 | async-start | bytes 524288 | tf_op jit(solution)/shard_map/psum | solution.py:12
  311.7 5.9 %copy-start.2 = (f32[128,512]{1,0:T(8,128)S(1)}, f32[128,512]{1,0:T(8,128)}, u32[]{:S(2)}) copy-start(f32[128,512]{1,0:T(8,128)} %all-reduce.6.cloned.1.call-done) | copy-start | bytes 786436
Sparse Core Ops, SparseCore 0:
  147.3 71.4 all-reduce.3
  241.2 70.4 all-reduce.5
  317.8 70.1 all-reduce.7
where the time goes:
time: 425 us; the launch traced here: 420 us
  waiting for transfers between devices  128 us (30%)
  other arithmetic  126 us (30%)
  matrix products  95.1 us (22%)
  local copies, waits for them, and re-layouts  48 us (11%)
  between operations  13.8 us (3%)
  starting transfers between devices  8.67 us (2%)
    another operation x5, other arithmetic, solve_panel(): jax.scipy.linalg.solve_triangular(diagonal, current[:, :PANEL].T, lower=T...  122 us
    psum x3, waiting for transfers between devices, spread(): return lax.psum(kept, axis)  96.6 us
    dot_general x6, matrix products, panel_product(): lax.dot_general(solved, panel_cols, (((1,), (1,)), ((), ())), precision=l...  72.3 us
    all_to_all x1, waiting for transfers between devices, per_device(): lax.all_to_all(outgoing, ('feat', 'pair'), split_axis=0, concat_axis=1, t...  31.2 us
    another operation x49, local copies, waits for them, and re-layouts, solve_panel(): jax.scipy.linalg.solve_triangular(diagonal, current[:, :PANEL].T, lower=T...  27.4 us
    reshape x2, local copies, waits for them, and re-layouts, per_device(): gradients = gradients.reshape(n_pair, per_group, n_feat, row_count)  11.9 us
    dot_general x1, matrix products, per_device(): jnp.einsum('ksti,kstj->kij', signed, in_factors, preferred_element_type=j...  9.84 us
  transfers between devices with their start and end apart: 4, of which 3 were waited for; matrix products, arithmetic and copies ran while one was open for 46% of the time, Pallas kernels for 0%

commit v1 on v0

--- a/solution.py
+++ b/solution.py
@@ -5,6 +5,13 @@
 
 PANEL = 512
 PANELS = 3
+
+
+def exchange_blocks(block, name, split, join):
+    count = lax.axis_size(name)
+    pieces = jnp.stack(jnp.split(block, count, axis=split), axis=0)
+    pieces = lax.all_to_all(pieces, name, split_axis=0, concat_axis=0)
+    return jnp.concatenate(pieces, axis=join)
 
 
 def spread(value, axis, source):
@@ -40,9 +47,7 @@
     group_pairs = slot_pair[0]
     pair_total = n_pair * n_feat * per_group
     outgoing = gradients.transpose(2, 0, 1, 3).reshape(n_feat * n_pair, per_group, row_count)
-    received = lax.all_to_all(
-        outgoing, ("feat", "pair"), split_axis=0, concat_axis=1, tiled=True
-    ).reshape(pair_total, row_count)
+    received = exchange_blocks(outgoing, ("feat", "pair"), 0, 1).reshape(pair_total, row_count)
     pair_rows = lax.broadcasted_iota(jnp.int32, (pair_total, pair_total), 0)
     placement = (pair_rows == group_pairs[None, :]).astype(jnp.float32)
     right_side = jnp.dot(

time: 425 us -> 445 us (1.047)
  local copies, waits for them, and re-layouts: 48 us -> 67.2 us
    unnamed x13 -> x44, local copies, waits for them, and re-layouts: 3.47 us -> 24 us
    another operation x0 -> x2, local copies, waits for them, and re-layouts: none -> 5.94 us  [the longest x1 5.27 us: per_device(): exchange_blocks(outgoing, ('feat', 'pair'), 0, 1)]
    reshape x1 -> x0, local copies, waits for them, and re-layouts: 5.27 us -> none  [per_device(): received = lax.all_to_all(outgoing, ('feat', 'pair'), split_axis=0, conca...]
  transfers between devices with their start and end apart: 4 -> 4, of which waited for: 3 -> 3; matrix products, arithmetic and copies ran while one was open for 46% -> 44% of each run, Pallas kernels for 0% -> 0%
where the time goes in v1:
time: 445 us; the launch traced here: 439 us
  waiting for transfers between devices  128 us (29%)
  other arithmetic  126 us (28%)
  matrix products  95 us (21%)
  local copies, waits for them, and re-layouts  67.2 us (15%)
  between operations  13.8 us (3%)
  starting transfers between devices  8.67 us (2%)
    another operation x5, other arithmetic, solve_panel(): jax.scipy.linalg.solve_triangular(diagonal, current[:, :PANEL].T, lower=T...  122 us
    psum x3, waiting for transfers between devices, spread(): return lax.psum(kept, axis)  96.7 us
    dot_general x6, matrix products, panel_product(): lax.dot_general(solved, panel_cols, (((1,), (1,)), ((), ())), precision=l...  72.3 us
    all_to_all x1, waiting for transfers between devices, exchange_blocks(): pieces = lax.all_to_all(pieces, name, split_axis=0, concat_axis=0)  31.2 us
    another operation x49, local copies, waits for them, and re-layouts, solve_panel(): jax.scipy.linalg.solve_triangular(diagonal, current[:, :PANEL].T, lower=T...  27.4 us
    unnamed x44, local copies, waits for them, and re-layouts  24 us
    dot_general x1, matrix products, per_device(): jnp.einsum('ksti,kstj->kij', signed, in_factors, preferred_element_type=j...  9.84 us
    reshape x2, local copies, waits for them, and re-layouts, per_device(): gradients = gradients.reshape(n_pair, per_group, n_feat, row_count)  9.84 us
  transfers between devices with their start and end apart: 4, of which 3 were waited for; matrix products, arithmetic and copies ran while one was open for 44% of the time, Pallas kernels for 0%

profile of v1, /device:TPU:0, one launch (start us, length us, event | category | flops | bytes accessed | tf_op | source)
XLA Modules:
  0.0 439.3 jit_solution(14972404944218895282)
XLA Ops:
  6.5 0.8 copy.20
  7.4 9.8 %fusion.18 = f32[16,256,256]{2,1,0:T(8,128)} fusion(bf16[16,2,512,256]{3,2,1,0:T(8,128)(2,1)} %param.7, bf16[16,2,512,256]{3,2,1,0:T(8,128)(2,1)} %param.8, bf16[16,2,512]{2,1,0:T(2,128)(2,1)S(1)} %fusion.95), kind=kOutput, calls=%fused_computation.19 | convolution fusion | flops 2151677952 | bytes 21004288 | tf_op jit(solution)/shard_map/ksti,kstj->kij/dot_general | solution.py:45
  17.3 5.0 %reshape.21 = f32[4,4,8,8192]{3,2,1,0:T(8,128)} reshape(f32[16,256,256]{2,1,0:T(8,128)} %fusion.18) | data formatting | bytes 8388608 | tf_op jit(solution)/shard_map/reshape | solution.py:46
  22.2 4.9 %copy.22 = f32[4,4,8,8192]{3,1,0,2:T(4,128)S(1)} copy(f32[4,4,8,8192]{3,2,1,0:T(8,128)} %reshape.21) | data formatting | bytes 8388608 | tf_op jit(solution)/shard_map/reshape | solution.py:46
  27.1 0.7 fusion.85
  29.1 0.7 fusion.82
  30.4 0.7 fusion.80
  31.7 0.7 fusion.78
  48.4 7.5 %all-to-all-start = ((f32[32,1,4,8192]{3,2,1,0:T(4,128)}), f32[32,1,4,8192]{3,2,1,0:T(4,128)}, u32[]{:S(2)}, u32[]{:S(2)}) async-start(f32[32,1,4,8192]{3,2,1,0:T(4,128)} %fusion.54), calls=%async_computation | async-start | bytes 8388608 | tf_op jit(solution)/shard_map/all_to_all | solution.py:13
  56.2 2.3 fusion.24
  58.5 8.4 %while.6 = (s32[]{:T(128)}, f32[512,512]{1,0:T(8,128)S(1)}, s32[4,2]{0,1:T(2,128)S(1)}, f32[4,128,128]{2,1,0:T(8,128)S(1)}, s32[]{:T(128)}) while((s32[]{:T(128)}, f32[512,512]{1,0:T(8,128)S(1)}, s32[4,2]{0,1:T(2,128)S(1)}, f32[4,128,128]{2,1,0:T(8,128)S(1)}, s32[]{:T(128)}) %tuple.51), condition=%wide.while_cond, body=%wide.while_body.sunk | while | flops 2 | bytes 131181 | solution.py:62
  59.2 1.4 bitcast_dynamic-update-slice_fusion.6
  61.3 1.4 bitcast_dynamic-update-slice_fusion.6
  63.4 1.4 bitcast_dynamic-update-slice_fusion.6
  65.6 1.4 bitcast_dynamic-update-slice_fusion.6
  67.0 0.7 copy-done.4
  67.7 40.1 %custom-call.5 = f32[4,128,128]{1,2,0:T(8,128)S(1)} custom-call(f32[4,128,128]{2,1,0:T(8,128)} %copy-done.4), custom_call_target="InvertDiagBlocksLowerTriangular" | custom-call | tf_op jit(solution)/shard_map/jit(_solve_triangular)/triangular_solve | solution.py:62
  107.8 0.8 broadcast.62.clone.1
  108.6 9.7 %while.7 = (s32[]{:T(128)}, f32[512,512]{1,0:T(8,128)S(1)}, s32[4,2]{0,1:T(2,128)S(1)}, f32[4,128,128]{2,1,0:T(8,128)}, s32[]{:T(128)}) while((s32[]{:T(128)}, f32[512,512]{1,0:T(8,128)S(1)}, s32[4,2]{0,1:T(2,128)S(1)}, f32[4,128,128]{2,1,0:T(8,128)}, s32[]{:T(128)}) %tuple.66), condition=%wide.while_cond.clone, body=%wide.while_body.clone.sunk | while | flops 2 | bytes 132705 | solution.py:62
  109.2 1.8 bitcast_dynamic-update-slice_fusion.7
  111.6 1.8 bitcast_dynamic-update-slice_fusion.7
  114.0 1.8 bitcast_dynamic-update-slice_fusion.7
  116.4 1.8 bitcast_dynamic-update-slice_fusion.7
  118.3 31.2 %all-to-all-done = f32[32,1,4,8192]{3,2,1,0:T(4,128)} async-done(((f32[32,1,4,8192]{3,2,1,0:T(4,128)}), f32[32,1,4,8192]{3,2,1,0:T(4,128)}, u32[]{:S(2)}, u32[]{:S(2)}) %all-to-all-start) | async-done | bytes 4194336 | tf_op jit(solution)/shard_map/all_to_all | solution.py:13
  149.5 5.3 %reshape_reshape.3 = f32[128,8192]{1,0:T(8,128)} reshape(f32[32,1,4,8192]{3,2,1,0:T(4,128)} %all-to-all-done) | data formatting | bytes 8388608 | tf_op jit(solution)/shard_map/reshape;reshape | solution.py:50
  154.8 4.5 %fusion.114 = f32[128,8192]{1,0:T(8,128)S(1)} fusion(f32[128,8192]{1,0:T(8,128)} %reshape_reshape.3, s32[128]{0:T(128)S(1)} %bitcast.271), kind=kOutput, calls=%fused_computation.180 | convolution fusion | flops 1610629120 | bytes 8389120 | tf_op jit(solution)/shard_map/dot_general | solution.py:53
  159.3 2.0 copy-done
  162.7 1.1 fusion.109
  164.6 1.1 fusion.108
  165.6 0.7 fusion.30
  167.1 7.8 %while.8 = (s32[]{:T(128)}, f32[512,512]{1,0:T(8,128)S(1)}, s32[4,2]{0,1:T(2,128)S(1)}, f32[4,128,128]{2,1,0:T(8,128)S(1)}, s32[]{:T(128)}) while((s32[]{:T(128)}, f32[512,512]{1,0:T(8,128)S(1)}, s32[4,2]{0,1:T(2,128)S(1)}, f32[4,128,128]{2,1,0:T(8,128)S(1)}, s32[]{:T(128)}) %tuple.67), condition=%wide.while_cond.clone.1, body=%wide.while_body.clone.1.sunk | while | flops 2 | bytes 131181 | solution.py:62
  167.7 1.3 bitcast_dynamic-update-slice_fusion.8
  169.7 1.3 bitcast_dynamic-update-slice_fusion.8
  171.6 1.3 bitcast_dynamic-update-slice_fusion.8
  173.6 1.3 bitcast_dynamic-update-slice_fusion.8
  174.9 40.1 %custom-call.6 = f32[4,128,128]{1,2,0:T(8,128)S(1)} custom-call(f32[4,128,128]{2,1,0:T(8,128)} %get-tuple-element.27), custom_call_target="InvertDiagBlocksLowerTriangular" | custom-call | tf_op jit(solution)/shard_map/jit(_solve_triangular)/triangular_solve | solution.py:62
  215.0 39.3 %custom-call.7 = f32[4,128,128]{1,2,0:T(8,128)S(1)} custom-call(f32[4,128,128]{2,1,0:T(8,128)S(1)} %get-tuple-element.28), custom_call_target="InvertDiagBlocksLowerTriangular" | custom-call | tf_op jit(solution)/shard_map/jit(_solve_triangular)/triangular_solve | solution.py:62
  254.4 2.6 fusion.23
  259.6 0.7 fusion.31
  260.6 21.2 %fusion.6 = f32[128,7680]{1,0:T(8,128)} fusion(f32[128,512]{1,0:T(8,128)S(1)} %copy-done.1, f32[8192,1536]{1,0:T(8,128)} %param.11, f32[128,8192]{1,0:T(8,128)} %copy-done), kind=kOutput, calls=%fused_computation.12 | convolution fusion | flops 6040780800 | bytes 23855104 | tf_op jit(solution)/shard_map/dot_general | solution.py:23
  281.8 49.3 %all-reduce.6.cloned.1.call-done = f32[128,512]{1,0:T(8,128)} async-done(((f32[128,512]{1,0:T(8,128)}), f32[128,512]{1,0:T(8,128)}) %all-reduce.6.cloned.1.call-update) | async-done | bytes 262160 | tf_op jit(solution)/shard_map/psum | solution.py:19
  331.0 2.6 fusion.22
  336.2 0.7 fusion.32
  336.9 23.0 %fusion.9 = f32[128,7680]{1,0:T(8,128)} fusion(f32[128,7680]{1,0:T(8,128)} %fusion.6, f32[128,512]{1,0:T(8,128)S(1)} %copy-done.2, f32[8192,1536]{1,0:T(8,128)} %param.11), kind=kOutput, calls=%fused_computation.13 | convolution fusion | flops 6040780800 | bytes 23855104 | tf_op jit(solution)/shard_map/dot_general | solution.py:23
  359.9 47.4 %all-reduce.8.cloned.1.call-done = f32[128,512]{1,0:T(8,128)} async-done(((f32[128,512]{1,0:T(8,128)}), f32[128,512]{1,0:T(8,128)}) %all-reduce.8.cloned.1.call-update) | async-done | bytes 262160 | tf_op jit(solution)/shard_map/psum | solution.py:19
  407.3 2.5 fusion.21
  409.8 20.4 %fusion.12 = f32[128,7680]{1,0:T(8,128)S(1)} fusion(f32[128,7680]{1,0:T(8,128)} %fusion.9, f32[128,512]{1,0:T(8,128)} %all-reduce.8.cloned.1.call-done, f32[8192,1536]{1,0:T(8,128)} %param.11), kind=kOutput, calls=%fused_computation.14 | convolution fusion | flops 6040780800 | bytes 23855104 | tf_op jit(solution)/shard_map/dot_general | solution.py:23
  430.2 2.3 pad_maximum_fusion
  (104 shorter events, 34.8 us)
Async XLA Ops:
  48.4 101.2 %all-to-all-start = ((f32[32,1,4,8192]{3,2,1,0:T(4,128)}), f32[32,1,4,8192]{3,2,1,0:T(4,128)}, u32[]{:S(2)}, u32[]{:S(2)}) async-start(f32[32,1,4,8192]{3,2,1,0:T(4,128)} %fusion.54), calls=%async_computation | async-start | bytes 8388608 | tf_op jit(solution)/shard_map/all_to_all | solution.py:13
  55.8 198.5 %all-reduce.4.cloned.1.call-start = ((), (), s32[]{:S(2)}) async-start(), calls=%async_computation.1 | async-start | bytes 524288 | tf_op jit(solution)/shard_map/psum | solution.py:19
  67.0 0.7 copy-start.4
  107.8 54.2 %copy-start.3 = (f32[4,128,128]{1,2,0:T(8,128)}, f32[4,128,128]{1,2,0:T(8,128)S(1)}, u32[]{:S(2)}) copy-start(f32[4,128,128]{1,2,0:T(8,128)S(1)} %custom-call.5) | copy-start | bytes 786436
  118.3 36.5 %copy-start.5 = (s32[1,128]{1,0:T(1,128)S(1)}, s32[1,128]{1,0:T(1,128)}, u32[]{:S(2)}) copy-start(s32[1,128]{1,0:T(1,128)} %param.10) | copy-start | bytes 1540
  159.3 2.0 copy-start
  166.4 164.6 %all-reduce.6.cloned.1.call-start = ((), (), s32[]{:S(2)}) async-start(), calls=%async_computation.2 | async-start | bytes 524288 | tf_op jit(solution)/shard_map/psum | solution.py:19
  254.4 6.2 %copy-start.1 = (f32[128,512]{1,0:T(8,128)S(1)}, f32[128,512]{1,0:T(8,128)}, u32[]{:S(2)}) copy-start(f32[128,512]{1,0:T(8,128)} %all-reduce.4.cloned.1.call-done) | copy-start | bytes 786436
  260.3 147.0 %all-reduce.8.cloned.1.call-start = ((), (), s32[]{:S(2)}) async-start(), calls=%async_computation.3 | async-start | bytes 524288 | tf_op jit(solution)/shard_map/psum | solution.py:19
  331.0 5.9 %copy-start.2 = (f32[128,512]{1,0:T(8,128)S(1)}, f32[128,512]{1,0:T(8,128)}, u32[]{:S(2)}) copy-start(f32[128,512]{1,0:T(8,128)} %all-reduce.6.cloned.1.call-done) | copy-start | bytes 786436
Sparse Core Ops, SparseCore 0:
  166.5 71.4 all-reduce.3
  260.5 70.5 all-reduce.5
  337.0 70.2 all-reduce.7
